TPU v7x, 32 devices: a whole 2x2x4 slice. The times are simulated.
32 devices in a mesh: dp: 16 (over z, y, x), mp: 2 (over core).
Axes of the slice: x: 2, y: 2, z: 4, core: 2. Of those that a mesh axis runs over, the one named last changes fastest.
Arguments:
- store_rows: bfloat16 [8192, 4096], P('dp', 'mp'), may hold values from -64 to 64
- norm_gain: bfloat16 [4096], replicated, may hold values from 0.099609375 to 1.8984375
- key_weight: bfloat16 [4096, 2048], P(None, 'mp'), may hold values from -0.09375 to 0.09375
- value_weight: bfloat16 [4096, 2048], P(None, 'mp'), may hold values from -0.09375 to 0.09375
- queries: bfloat16 [128, 2048], P('dp', 'mp'), may hold values from -300 to 300
- counts: int32 [16], replicated, may hold values from 1 to 8, 32 in all
- slot_plan: int32 [32], P('dp'), may hold values from 0 to 31, each once
Outputs:
- context: bfloat16 [128, 2048], P('dp', 'mp')
All inputs are finite; a program needn't handle non-finite values.
Results may differ from a plain program's by a relative error of at most 0.0091.
Values may be sent and summed in bfloat16 or wider, within the bound.
A program may use at most 64 MiB of HBM per device.

v0:
```python
import jax
import jax.numpy as jnp
from jax import lax
from jax.sharding import PartitionSpec as P

HEAD_DIM = 64


norm_eps = 1e-06
score_scale = 0.125
far_below = -1e30


def local(store_rows, norm_gain, key_weight, value_weight, queries, counts, slot_plan):
    full_width = norm_gain.shape[0]
    row_count = store_rows.shape[0]
    local_cols = store_rows.shape[1]
    head_cols = key_weight.shape[1]
    heads_here = head_cols // HEAD_DIM
    passages_here = slot_plan.shape[0]
    seq_len = row_count // passages_here
    gain_full = norm_gain.astype(jnp.float32)
    raw_rows = store_rows.astype(jnp.float32)
    own_gain = lax.dynamic_slice_in_dim(gain_full, lax.axis_index("mp") * local_cols, local_cols, 0)
    scaled = (raw_rows * own_gain[None, :]).astype(jnp.bfloat16)
    total_sq = lax.psum(jnp.sum(raw_rows * raw_rows, axis=1), "mp")
    shard_part = lax.all_gather(scaled, "mp", axis=1, tiled=True)
    key_acc = jnp.dot(shard_part, key_weight, preferred_element_type=jnp.float32)
    value_acc = jnp.dot(shard_part, value_weight, preferred_element_type=jnp.float32)
    inv_rms = lax.rsqrt(total_sq / full_width + norm_eps)
    key_rows = (key_acc * inv_rms[:, None]).astype(jnp.bfloat16)
    value_rows = (value_acc * inv_rms[:, None]).astype(jnp.bfloat16)
    ends = jnp.cumsum(counts)
    slot_question = jnp.sum((slot_plan[:, None] >= ends[None, :]).astype(jnp.int32), axis=1)
    num_questions = counts.shape[0]
    dec_len = queries.shape[0]
    gathered = lax.all_gather(queries, "dp", axis=0, tiled=True)
    query_table = gathered.reshape(num_questions, dec_len, heads_here, HEAD_DIM)
    slot_queries = jnp.take(query_table, slot_question, axis=0)
    key_blocks = key_rows.reshape(passages_here, seq_len, heads_here, HEAD_DIM)
    value_blocks = value_rows.reshape(passages_here, seq_len, heads_here, HEAD_DIM).astype(
        jnp.float32
    )
    scores = (
        jnp.einsum("pihd,pthd->piht", slot_queries, key_blocks, preferred_element_type=jnp.float32)
        * score_scale
    )
    slot_max = jnp.max(scores, axis=3)
    member = slot_question[None, :] == jnp.arange(num_questions, dtype=jnp.int32)[:, None]
    member_float = member.astype(jnp.float32)
    question_max = jnp.max(jnp.where(member[:, :, None, None], slot_max[None], far_below), axis=1)
    max_level = lax.pmax(question_max, "dp")
    slot_level = jnp.take(max_level, slot_question, axis=0)
    weights = jnp.exp(scores - slot_level[..., None])
    slot_den = jnp.sum(weights, axis=3)
    slot_num = jnp.einsum("piht,pthd->pihd", weights, value_blocks, precision=lax.Precision.HIGHEST)
    slot_num = slot_num.reshape(passages_here, dec_len, head_cols)
    numerator = jnp.einsum("qp,pik->qik", member_float, slot_num, precision=lax.Precision.HIGHEST)
    denominator = jnp.einsum("qp,pih->qih", member_float, slot_den, precision=lax.Precision.HIGHEST)
    numerator, denominator = (numerator, denominator)
    summed_num, summed_den = (
        lax.psum_scatter(numerator, "dp", scatter_dimension=0, tiled=True),
        lax.psum_scatter(denominator, "dp", scatter_dimension=0, tiled=True),
    )
    own_num = summed_num[0]
    own_den = summed_den[0]
    context = own_num.reshape(dec_len, heads_here, HEAD_DIM) / own_den[..., None]
    return context.reshape(dec_len, head_cols).astype(jnp.bfloat16)


def solution(mesh):
    placed = (P("dp", "mp"), P(), P(None, "mp"), P(None, "mp"), P("dp", "mp"), P(), P("dp"))
    return jax.shard_map(
        local, mesh=mesh, in_specs=placed, out_specs=P("dp", "mp"), check_vma=False
    )
```

profile of v0, /device:TPU:0, one launch (start us, length us, event | category | flops | bytes accessed | tf_op | source)
XLA Modules:
  0.0 241.7 jit_solution(15678639214267508043)
XLA Ops:
  6.5 0.7 dynamic-slice_convert_fusion
  7.2 3.5 %fusion.1 = (f32[512]{0:T(512)S(1)}, bf16[512,2048]{1,0:T(8,128)(2,1)}) fusion(bf16[512,2048]{1,0:T(8,128)(2,1)} %param.7, f32[2048]{0:T(1024)S(1)} %dynamic-slice_convert_fusion), kind=kLoop, calls=%fused_computation.5 | loop fusion | flops 5242368 | bytes 4204544 | tf_op jit(solution)/shard_map/reduce_sum | solution.py:26
  10.8 0.6 copy-done.1
  11.4 0.1 copy.36
  11.5 0.1 reduce
  11.7 0.2 fusion.23
  11.8 0.1 iota_compare_fusion
  11.9 0.1 copy.41
  12.0 43.8 %all_gather.7 = bf16[128,1024]{1,0:T(8,128)(2,1)S(1)} all-gather(bf16[8,1024]{1,0:T(8,128)(2,1)S(1)} %copy-done), channel_id=1, replica_groups=mesh['dp'=16,'mp'=2] {'dp'}, dimensions={0}, use_global_device_ids=true | all-gather | bytes 278528 | tf_op jit(solution)/shard_map/all_gather | solution.py:37
  55.8 0.3 reshape.86
  56.2 0.6 gather_fusion
  56.7 2.5 %psum.7 = f32[512]{0:T(512)S(1)} all-reduce(f32[512]{0:T(512)S(1)} %get-tuple-element.5), channel_id=1, replica_groups=mesh['dp'=16,'mp'=2] {'mp'}, use_global_device_ids=true, to_apply=%region_3.4 | all-reduce | flops 512 | bytes 4096 | tf_op jit(solution)/shard_map/psum | solution.py:26
  59.2 0.1 broadcast_select_fusion
  59.3 9.1 %multiply_convert_fusion.1 = bf16[512,1024]{1,0:T(8,128)(2,1)S(1)} fusion(bf16[512,4096]{1,0:T(8,128)(2,1)} %all-gather.2.cloned.1.call-done, bf16[4096,1024]{1,0:T(8,128)(2,1)} %param.10, f32[512]{0:T(512)S(1)} %add_rsqrt_fusion), kind=kOutput, calls=%fused_computation.11 | convolution fusion | flops 4296015872 | bytes 13633536 | tf_op jit(solution)/shard_map/dot_general | solution.py:29
  68.4 1.3 reshape.105
  69.8 9.1 %multiply_convert_fusion = bf16[512,1024]{1,0:T(8,128)(2,1)S(1)} fusion(bf16[512,4096]{1,0:T(8,128)(2,1)} %all-gather.2.cloned.1.call-done, bf16[4096,1024]{1,0:T(8,128)(2,1)} %param.9, f32[512]{0:T(512)S(1)} %add_rsqrt_fusion), kind=kOutput, calls=%fused_computation.10 | convolution fusion | flops 4296015872 | bytes 13633536 | tf_op jit(solution)/shard_map/dot_general | solution.py:28
  78.9 2.4 reshape.106
  81.3 2.3 fusion.25
  83.7 0.1 select_reduce_fusion
  83.8 72.0 %pmax.7 = f32[16,8,16]{2,1,0:T(8,128)S(1)} all-reduce(f32[16,8,16]{2,1,0:T(8,128)S(1)} %select_reduce_fusion), channel_id=1, replica_groups=mesh['dp'=16,'mp'=2] {'dp'}, use_global_device_ids=true, to_apply=%region_6.7 | all-reduce | flops 2048 | bytes 16384 | tf_op jit(solution)/shard_map/pmax | solution.py:52
  155.8 0.5 gather_fusion.1
  156.5 1.2 fusion.12
  157.8 0.1 reshape.107
  157.9 0.5 fusion.21
  158.4 1.1 copy.47
  159.5 0.6 dynamic-slice
  160.1 0.2 fusion.15
  160.4 0.3 fusion.19
  160.7 71.9 %all-reduce = f32[16,8,16]{2,1,0:T(8,128)S(1)} all-reduce(f32[16,8,16]{2,1,0:T(8,128)S(1)} %copy.49), channel_id=3, replica_groups=mesh['dp'=16,'mp'=2] {'dp'}, use_global_device_ids=true, to_apply=%region_9.10.clone | all-reduce | flops 2048 | bytes 16384
  232.7 0.6 dynamic-slice_bitcast_fusion
  233.4 0.1 div.23
  233.5 1.4 fusion.18
  (25 shorter events, 0.6 us)
Async XLA Ops:
  6.5 52.8 %all-gather.2.cloned.1.call-start = ((), (), s32[]{:S(2)}) async-start(), calls=%async_computation.1 | async-start | bytes 6291456 | tf_op jit(solution)/shard_map/all_gather | solution.py:27
  10.8 0.7 copy-start.1
  10.8 0.9 copy-start.2
  10.8 1.3 copy-start
  10.8 222.7 %reduce-scatter.2.cloned.1.call-start = ((), (), s32[]{:S(2)}) async-start(), calls=%async_computation.2 | async-start | bytes 557056 | tf_op jit(solution)/shard_map/reduce_scatter | solution.py:62
  157.7 1.8 copy-start.3
Sparse Core Ops, SparseCore 0:
  10.9 16.3 all-gather.1
  159.6 72.4 reduce-scatter.1
where the time goes:
time: 242 us
  blocking collectives  190 us (79%)
  matrix products  22.6 us (9%)
  between operations  13.5 us (6%)
  local copies, waits for them, and re-layouts  8.82 us (4%)
  other arithmetic  6.49 us (3%)
    pmax x1, blocking collectives, local(): max_level = lax.pmax(question_max, 'dp')  72 us
    unnamed x1, blocking collectives  71.9 us
    all_gather x1, blocking collectives, local(): gathered = lax.all_gather(queries, 'dp', axis=0, tiled=True)  43.8 us
    dot_general x1, matrix products, local(): jnp.dot(shard_part, key_weight, preferred_element_type=jnp.float32)  9.15 us
    dot_general x1, matrix products, local(): jnp.dot(shard_part, value_weight, preferred_element_type=jnp.float32)  9.15 us
  transfers between devices with their start and end apart: 2, of which 0 were waited for; matrix products, arithmetic and copies ran while one was open for 1% of the time, Pallas kernels for 0%

commit v1 on v0

v1 whole, which is shorter than its diff:
```python
import functools

import jax
import jax.numpy as jnp
from jax import lax
from jax.experimental import pallas as pl
from jax.experimental.pallas import tpu as pltpu
from jax.sharding import PartitionSpec as P

HEAD_DIM = 64
MESH = pl.DeviceIdType.MESH

norm_eps = 1e-06
score_scale = 0.125
far_below = -1e30


def body(dims, counts, plan, gain, queries, rows_hbm, key_hbm, value_hbm, out,
         raw, scaled, wbuf, acc, kvb, sumsq, qbuf, part, stat, sbuf, rbuf,
         rows_sem, w_sem, rsend, rrecv, qsend, qrecv, osend, orecv):
    dp, mp, row_count, feats, cols, width, questions, dec, passages = dims
    full = feats * mp
    seq = row_count // passages
    groups = cols // width
    chunks = 2 * groups
    heads = cols // HEAD_DIM
    gheads = width // HEAD_DIM
    me = lax.axis_index("dp")
    core = lax.axis_index("mp")

    own_rows = pltpu.make_async_copy(rows_hbm, raw.at[0], rows_sem)
    own_rows.start()

    def weight_copy(s, c):
        owner = lax.rem(core + s, mp)
        source = key_hbm if c < groups else value_hbm
        at = (c % groups) * width
        return pltpu.make_async_copy(
            source.at[pl.ds(pl.multiple_of(owner * feats, feats), feats), pl.ds(at, width)],
            wbuf.at[s, c], w_sem.at[s, c])

    for s in range(mp):
        for c in range(chunks):
            weight_copy(s, c).start()

    barrier = pltpu.get_barrier_semaphore()
    for j in range(1, dp):
        pl.semaphore_signal(barrier, inc=1, device_id=(lax.rem(me + j, dp), core), device_id_type=MESH)
    for s in range(1, mp):
        pl.semaphore_signal(barrier, inc=1, device_id=(me, lax.rem(core + s, mp)), device_id_type=MESH)
    pl.semaphore_wait(barrier, dp - 1 + mp - 1)

    row_copies = []
    for s in range(1, mp):
        row_copies.append(pltpu.make_async_remote_copy(
            src_ref=rows_hbm, dst_ref=raw.at[s], send_sem=rsend.at[s], recv_sem=rrecv.at[s],
            device_id=(me, lax.rem(core + mp - s, mp)), device_id_type=MESH))
        row_copies[-1].start()
    query_copies = []
    for j in range(1, dp):
        query_copies.append(pltpu.make_async_remote_copy(
            src_ref=queries, dst_ref=qbuf.at[me], send_sem=qsend.at[j], recv_sem=qrecv.at[j],
            device_id=(lax.rem(me + j, dp), core), device_id_type=MESH))
        query_copies[-1].start()
    qbuf[me] = queries[...]

    row_step = 64

    def scale(s):
        owner = lax.rem(core + s, mp)
        own_gain = gain[:, pl.ds(pl.multiple_of(owner * feats, feats), feats)].astype(jnp.float32)

        def step(i, carry):
            at = pl.ds(pl.multiple_of(i * row_step, row_step), row_step)
            x = raw[s, at, :].astype(jnp.float32)
            scaled[s, at, :] = (x * own_gain).astype(jnp.bfloat16)
            total = jnp.sum(x * x, axis=1, keepdims=True)
            if s > 0:
                total = total + sumsq[at, :]
            sumsq[at, :] = total
            return carry

        lax.fori_loop(0, row_count // row_step, step, 0)

    own_rows.wait()
    for s in range(mp):
        if s > 0:
            row_copies[s - 1].wait()
        scale(s)
        if s == mp - 1:
            inv_rms = lax.rsqrt(sumsq[...] * (1.0 / full) + norm_eps)
        for c in range(chunks):
            weight_copy(s, c).wait()
            product = jnp.dot(scaled[s], wbuf[s, c], preferred_element_type=jnp.float32)
            if s > 0:
                product = product + acc[c]
            if s == mp - 1:
                kvb[c] = (product * inv_rms).astype(jnp.bfloat16)
            else:
                acc[c] = product

    for copy in query_copies:
        copy.wait()

    slot = []
    for p in range(passages):
        plan_p = plan[p]

        def count(q, carry):
            end, total = carry
            end = end + counts[q]
            return end, total + jnp.where(end <= plan_p, 1, 0)

        found = lax.fori_loop(0, questions, count, (jnp.int32(0), jnp.int32(0)))[1]
        slot.append(jnp.minimum(found, questions - 1))
    same = [[slot[a] == slot[b] for b in range(passages)] for a in range(passages)]

    tall = gheads * dec
    row_head = lax.broadcasted_iota(jnp.int32, (tall, width), 0) // dec
    col_head = lax.broadcasted_iota(jnp.int32, (tall, width), 1) // HEAD_DIM
    diagonal = row_head == col_head
    stat_row = lax.broadcasted_iota(jnp.int32, (tall, 128), 0) // dec
    stat_lane = lax.broadcasted_iota(jnp.int32, (tall, 128), 1)
    own_queries = [qbuf[slot[p]].astype(jnp.float32) for p in range(passages)]

    stats = [jnp.zeros((dec, 128), jnp.float32) for _ in range(passages)]
    for g in range(groups):
        scores, tops = [], []
        for p in range(passages):
            q = own_queries[p][:, g * width:(g + 1) * width]
            q = jnp.where(diagonal, jnp.concatenate([q] * gheads, axis=0), 0.0).astype(jnp.bfloat16)
            k = kvb[g, p * seq:(p + 1) * seq, :]
            s = lax.dot_general(q, k, (((1,), (1,)), ((), ())), preferred_element_type=jnp.float32) * score_scale
            scores.append(s)
            tops.append(jnp.max(s, axis=1, keepdims=True))
        nums, dens, levels = [], [], []
        for p in range(passages):
            level = tops[p]
            for o in range(passages):
                if o != p:
                    level = jnp.maximum(level, jnp.where(same[p][o], tops[o], far_below))
            w = jnp.exp(scores[p] - level)
            dens.append(jnp.sum(w, axis=1, keepdims=True))
            v = kvb[groups + g, p * seq:(p + 1) * seq, :]
            nums.append(jnp.dot(w.astype(jnp.bfloat16), v, preferred_element_type=jnp.float32))
            levels.append(level)
        for p in range(passages):
            num, den = nums[p], dens[p]
            for o in range(passages):
                if o != p:
                    num = num + jnp.where(same[p][o], nums[o], 0.0)
                    den = den + jnp.where(same[p][o], dens[o], 0.0)
            o_group = jnp.where(diagonal, num / den, 0.0)
            part[p, :, g * width:(g + 1) * width] = jnp.sum(o_group.reshape(gheads, dec, width), axis=0)
            lse = jnp.broadcast_to(levels[p] + jnp.log(den), (tall, 128))
            head = stat_row + g * gheads
            put = (stat_lane == head) | (stat_lane == head + heads) | (stat_lane == head + 2 * heads)
            stats[p] = stats[p] + jnp.sum(jnp.where(put, lse, 0.0).reshape(gheads, dec, 128), axis=0)
    lane = lax.broadcasted_iota(jnp.int32, (dec, 128), 1)
    for p in range(passages):
        high = stats[p].astype(jnp.bfloat16).astype(jnp.float32)
        rest = stats[p] - high
        middle = rest.astype(jnp.bfloat16).astype(jnp.float32)
        low = rest - middle
        stat[p] = jnp.where(lane < heads, high, jnp.where(lane < 2 * heads, middle, low))
    nothing = jnp.where(lane < heads, far_below, 0.0)

    def payload(dst):
        a = jnp.zeros((dec, cols), jnp.float32)
        b = nothing
        for p in range(passages):
            a = jnp.where(slot[p] == dst, part[p], a)
            b = jnp.where(slot[p] == dst, stat[p], b)
        return a.astype(jnp.bfloat16), b.astype(jnp.bfloat16)

    out_copies = []
    for j in range(1, dp):
        dst = lax.rem(me + j, dp)
        a, b = payload(dst)
        sbuf[j, :, :cols] = a
        sbuf[j, :, cols:] = b
        out_copies.append(pltpu.make_async_remote_copy(
            src_ref=sbuf.at[j], dst_ref=rbuf.at[me], send_sem=osend.at[j], recv_sem=orecv.at[j],
            device_id=(dst, core), device_id_type=MESH))
        out_copies[-1].start()
    a, b = payload(me)
    rbuf[me, :, :cols] = a
    rbuf[me, :, cols:] = b
    for copy in out_copies:
        copy.wait()

    pick_row = lax.broadcasted_iota(jnp.int32, (128, width), 0)
    pick_col = lax.broadcasted_iota(jnp.int32, (128, width), 1) // HEAD_DIM
    got = rbuf[:, :, cols:].astype(jnp.float32).reshape(dp * dec, 128).astype(jnp.bfloat16)
    for g in range(groups):
        head = pick_col + g * gheads
        pick = (pick_row == head) | (pick_row == head + heads) | (pick_row == head + 2 * heads)
        pick = jnp.where(pick, 1.0, 0.0).astype(jnp.bfloat16)
        lse = jnp.dot(got, pick, preferred_element_type=jnp.float32).reshape(dp, dec, width)
        share = jnp.exp(lse - jnp.max(lse, axis=0, keepdims=True))
        parts = rbuf[:, :, g * width:(g + 1) * width].astype(jnp.float32)
        total = jnp.sum(share * parts, axis=0) / jnp.sum(share, axis=0)
        out[:, g * width:(g + 1) * width] = total.astype(jnp.bfloat16)


def local(dp, mp, store_rows, norm_gain, key_weight, value_weight, queries, counts, slot_plan):
    row_count, feats = store_rows.shape
    cols = key_weight.shape[1]
    width = min(256, cols)
    passages = slot_plan.shape[0]
    dec = queries.shape[0]
    questions = counts.shape[0]
    chunks = 2 * cols // width
    dims = (dp, mp, row_count, feats, cols, width, questions, dec, passages)
    vmem = pl.BlockSpec(memory_space=pltpu.VMEM)
    smem = pl.BlockSpec(memory_space=pltpu.SMEM)
    hbm = pl.BlockSpec(memory_space=pl.ANY)
    bf16, f32 = jnp.bfloat16, jnp.float32
    dma = pltpu.SemaphoreType.DMA
    return pl.pallas_call(
        functools.partial(body, dims),
        out_shape=jax.ShapeDtypeStruct((dec, cols), bf16),
        in_specs=[smem, smem, vmem, vmem, hbm, hbm, hbm],
        out_specs=vmem,
        scratch_shapes=[
            pltpu.VMEM((mp, row_count, feats), bf16),
            pltpu.VMEM((mp, row_count, feats), bf16),
            pltpu.VMEM((mp, chunks, feats, width), bf16),
            pltpu.VMEM((chunks, row_count, width), f32),
            pltpu.VMEM((chunks, row_count, width), bf16),
            pltpu.VMEM((row_count, 1), f32),
            pltpu.VMEM((dp, dec, cols), bf16),
            pltpu.VMEM((passages, dec, cols), f32),
            pltpu.VMEM((passages, dec, 128), f32),
            pltpu.VMEM((dp, dec, cols + 128), bf16),
            pltpu.VMEM((dp, dec, cols + 128), bf16),
            dma(()),
            dma((mp, chunks)),
            dma((mp,)),
            dma((mp,)),
            dma((dp,)),
            dma((dp,)),
            dma((dp,)),
            dma((dp,)),
        ],
        compiler_params=pltpu.CompilerParams(
            collective_id=0, has_side_effects=True, vmem_limit_bytes=56 * 1024 * 1024),
    )(counts, slot_plan, norm_gain.reshape(1, -1), queries, store_rows, key_weight, value_weight)


def solution(mesh):
    placed = (P("dp", "mp"), P(), P(None, "mp"), P(None, "mp"), P("dp", "mp"), P(), P("dp"))
    return jax.shard_map(
        functools.partial(local, mesh.shape["dp"], mesh.shape["mp"]),
        mesh=mesh, in_specs=placed, out_specs=P("dp", "mp"), check_vma=False
    )
```

time: 242 us -> 45.8 us (0.19)
  blocking collectives: 190 us -> 0 us
  Pallas kernels: 0 us -> 42.8 us
  matrix products: 22.6 us -> 0 us
  between operations: 13.5 us -> 0.01 us
  other arithmetic: 6.49 us -> 0 us
  local copies, waits for them, and re-layouts: 8.82 us -> 2.64 us
    pmax x1 -> x0, blocking collectives: 72 us -> none  [local(): max_level = lax.pmax(question_max, 'dp')]
    unnamed x1 -> x0, blocking collectives: 71.9 us -> none
    all_gather x1 -> x0, blocking collectives: 43.8 us -> none  [local(): gathered = lax.all_gather(queries, 'dp', axis=0, tiled=True)]
    pallas_call x0 -> x1, Pallas kernels: none -> 42.8 us  [local(): pl.pallas_call(functools.partial(body, dims), out_shape=jax.ShapeDtypeStr...]
    dot_general x6 -> x0, matrix products: 22.6 us -> none  [the longest x1 9.15 us: local(): jnp.dot(shard_part, key_weight, preferred_element_type=jnp.float32)]
    reduce_sum x3 -> x0, other arithmetic: 3.91 us -> none  [the longest x1 3.53 us: local(): total_sq = lax.psum(jnp.sum(raw_rows * raw_rows, axis=1), 'mp')]
    reshape x5 -> x1, local copies, waits for them, and re-layouts: 4.2 us -> 1.31 us  [local(): norm_gain.reshape(1, -1)]
    psum x1 -> x0, blocking collectives: 2.47 us -> none  [local(): total_sq = lax.psum(jnp.sum(raw_rows * raw_rows, axis=1), 'mp')]
  transfers between devices with their start and end apart: 2 -> 0, of which waited for: 0 -> 0; matrix products, arithmetic and copies ran while one was open for 1% -> 0% of each run, Pallas kernels for 0% -> 0%
where the time goes in v1:
time: 45.8 us; the launch traced here: 45.4 us
  Pallas kernels  42.8 us (93%)
  local copies, waits for them, and re-layouts  2.64 us (6%)
    pallas_call x1, Pallas kernels, local(): pl.pallas_call(functools.partial(body, dims), out_shape=jax.ShapeDtypeStr...  42.8 us
    unnamed x1, local copies, waits for them, and re-layouts  1.32 us
    reshape x1, local copies, waits for them, and re-layouts, local(): norm_gain.reshape(1, -1)  1.31 us

profile of v1, /device:TPU:0, one launch (start us, length us, event | category | flops | bytes accessed | tf_op | source)
XLA Modules:
  0.0 45.4 jit_solution(9612240375084349480)
XLA Ops:
  0.0 1.3 %reshape.3.gain = bf16[1,4096]{1,0:T(2,128)(2,1)} reshape(bf16[4096]{0:T(1024)(128)(2,1)} %param.8) | data formatting | bytes 16384 | tf_op jit(solution)/shard_map/reshape | solution.py:248
  1.3 42.8 %shard_map.73 = bf16[8,1024]{1,0:T(8,128)(2,1)} custom-call(s32[16]{0:T(128)} %counts.1, s32[2]{0:T(128)} %plan.1, bf16[1,4096]{1,0:T(2,128)(2,1)} %reshape.3.gain, bf16[8,1024]{1,0:T(8,128)(2,1)} %queries.1, bf16[512,2048]{1,0:T(8,128)(2,1)} %rows_hbm.1, bf16[4096,1024]{1,0:T(8,128)(2,1)} %key_hbm.1, bf16[4096,1024]{1,0:T(8,128)(2,1)} %value_hbm.1), custom_call_target="tpu_custom_call" | custom-call | tf_op jit(solution)/shard_map/pallas_call | solution.py:220
  44.1 1.3 %copy.9 = bf16[8,1024]{1,0:T(8,128)(2,1)} copy(bf16[8,1024]{1,0:T(8,128)(2,1)} %shard_map.73) | data formatting | bytes 32768

commit v2 on v1

v2 whole, which is shorter than its diff:
```python
import functools

import jax
import jax.numpy as jnp
from jax import lax
from jax.experimental import pallas as pl
from jax.experimental.pallas import tpu as pltpu
from jax.sharding import PartitionSpec as P

HEAD_DIM = 64
MESH = pl.DeviceIdType.MESH

norm_eps = 1e-06
score_scale = 0.125
far_below = -1e30


def body(dims, counts, plan, gain, queries, rows_hbm, key_hbm, value_hbm, out,
         raw, scaled, wbuf, acc, kvb, sumsq, qbuf, part1, stat1, part2, stat2, part3, stat3,
         rows_sem, w_sem, rsend, rrecv, qsend, qrecv, send1, recv1, send2, recv2):
    dp, mp, inner_count, row_count, feats, cols, piece, width, questions, dec, passages = dims
    full = feats * mp
    pieces = feats // piece
    seq = row_count // passages
    groups = cols // width
    gheads = width // HEAD_DIM
    outer_count = dp // inner_count
    me = lax.axis_index("dp")
    core = lax.axis_index("mp")
    inner = lax.rem(me, inner_count)
    outer = lax.div(me, inner_count)
    weights = (key_hbm, value_hbm)

    def feature_span(k):
        return pl.ds(k * piece, piece)

    def own_copy(k):
        return pltpu.make_async_copy(
            rows_hbm.at[:, feature_span(k)], raw.at[0, :, feature_span(k)], rows_sem.at[k])

    def weight_copy(s, k, c):
        start = lax.rem(core + s, mp) * feats + k * piece
        return pltpu.make_async_copy(
            weights[c].at[pl.ds(pl.multiple_of(start, piece), piece), :],
            wbuf.at[s, k, c], w_sem.at[s, k, c])

    for k in range(pieces):
        own_copy(k).start()
        for c in range(2):
            weight_copy(0, k, c).start()

    barrier = pltpu.get_barrier_semaphore()
    for s in range(1, mp):
        pl.semaphore_signal(barrier, inc=1, device_id=(me, lax.rem(core + s, mp)), device_id_type=MESH)
    for j in range(1, dp):
        pl.semaphore_signal(barrier, inc=1, device_id=(lax.rem(me + j, dp), core), device_id_type=MESH)
    pl.semaphore_wait(barrier, dp - 1 + mp - 1)

    def row_copy(s, k):
        return pltpu.make_async_remote_copy(
            src_ref=rows_hbm.at[:, feature_span(k)], dst_ref=raw.at[s, :, feature_span(k)],
            send_sem=rsend.at[s, k], recv_sem=rrecv.at[s, k],
            device_id=(me, lax.rem(core + mp - s, mp)), device_id_type=MESH)

    for s in range(1, mp):
        for k in range(pieces):
            row_copy(s, k).start()
    query_copies = []
    for j in range(1, dp):
        query_copies.append(pltpu.make_async_remote_copy(
            src_ref=queries, dst_ref=qbuf.at[me], send_sem=qsend.at[j], recv_sem=qrecv.at[j],
            device_id=(lax.rem(me + j, dp), core), device_id_type=MESH))
        query_copies[-1].start()
    for s in range(1, mp):
        for k in range(pieces):
            for c in range(2):
                weight_copy(s, k, c).start()
    qbuf[me] = queries[...]

    row_step = 64

    def scale(s, k):
        start = lax.rem(core + s, mp) * feats + k * piece
        own_gain = gain[:, pl.ds(pl.multiple_of(start, piece), piece)].astype(jnp.float32)

        def step(i, carry):
            at = pl.ds(pl.multiple_of(i * row_step, row_step), row_step)
            x = raw[s, at, feature_span(k)].astype(jnp.float32)
            scaled[at, :] = (x * own_gain).astype(jnp.bfloat16)
            total = jnp.sum(x * x, axis=1, keepdims=True)
            if s + k > 0:
                total = total + sumsq[at, :]
            sumsq[at, :] = total
            return carry

        lax.fori_loop(0, row_count // row_step, step, 0)

    for s in range(mp):
        for k in range(pieces):
            if s == 0:
                own_copy(k).wait()
            else:
                row_copy(s, k).wait()
            scale(s, k)
            last = s == mp - 1 and k == pieces - 1
            if last:
                inv_rms = lax.rsqrt(sumsq[...] * (1.0 / full) + norm_eps)
            for c in range(2):
                weight_copy(s, k, c).wait()
                product = jnp.dot(scaled[...], wbuf[s, k, c], preferred_element_type=jnp.float32)
                if s + k > 0:
                    product = product + acc[c]
                if last:
                    kvb[c] = (product * inv_rms).astype(jnp.bfloat16)
                else:
                    acc[c] = product

    for copy in query_copies:
        copy.wait()

    slot = []
    for p in range(passages):
        plan_p = plan[p]

        def count(q, carry):
            end, total = carry
            end = end + counts[q]
            return end, total + jnp.where(end <= plan_p, 1, 0)

        found = lax.fori_loop(0, questions, count, (jnp.int32(0), jnp.int32(0)))[1]
        slot.append(jnp.minimum(found, questions - 1))

    tall = gheads * dec
    row_head = lax.broadcasted_iota(jnp.int32, (tall, width), 0) // dec
    col_head = lax.broadcasted_iota(jnp.int32, (tall, width), 1) // HEAD_DIM
    diagonal = row_head == col_head
    stat_row = lax.broadcasted_iota(jnp.int32, (tall, 128), 0) // dec
    stat_lane = lax.broadcasted_iota(jnp.int32, (tall, 128), 1)

    for p in range(passages):
        own_queries = qbuf[slot[p]].astype(jnp.float32)
        stats = jnp.zeros((dec, 128), jnp.float32)
        for g in range(groups):
            at = slice(g * width, (g + 1) * width)
            q = own_queries[:, at]
            q = jnp.where(diagonal, jnp.concatenate([q] * gheads, axis=0), 0.0).astype(jnp.bfloat16)
            k = kvb[0, p * seq:(p + 1) * seq, at]
            scores = lax.dot_general(q, k, (((1,), (1,)), ((), ())), preferred_element_type=jnp.float32) * score_scale
            level = jnp.max(scores, axis=1, keepdims=True)
            w = jnp.exp(scores - level)
            den = jnp.sum(w, axis=1, keepdims=True)
            v = kvb[1, p * seq:(p + 1) * seq, at]
            num = jnp.dot(w.astype(jnp.bfloat16), v, preferred_element_type=jnp.float32)
            mine = jnp.where(diagonal, num / den, 0.0)
            part1[inner, p, :, at] = jnp.sum(mine.reshape(gheads, dec, width), axis=0).astype(jnp.bfloat16)
            lse = jnp.broadcast_to(level + jnp.log(den), (tall, 128))
            put = stat_lane == stat_row + g * gheads
            stats = stats + jnp.sum(jnp.where(put, lse, 0.0).reshape(gheads, dec, 128), axis=0)
        stat1[inner, p, 0] = stats
        stat1[inner, p, 1] = jnp.full((dec, 128), slot[p].astype(jnp.float32))

    copies1 = []
    for j in range(1, inner_count):
        target = (outer * inner_count + lax.rem(inner + j, inner_count), core)
        for i, buf in enumerate((part1, stat1)):
            copies1.append(pltpu.make_async_remote_copy(
                src_ref=buf.at[inner], dst_ref=buf.at[inner], send_sem=send1.at[i, j], recv_sem=recv1.at[i, j],
                device_id=target, device_id_type=MESH))
            copies1[-1].start()

    pick_row = lax.rem(lax.broadcasted_iota(jnp.int32, (256, cols), 0), 128)
    pick_col = lax.broadcasted_iota(jnp.int32, (256, cols), 1) // HEAD_DIM
    pick = jnp.where(pick_row == pick_col, 1.0, 0.0).astype(jnp.bfloat16)

    def merge(lse, hit, parts):
        n = lse.shape[0]
        lse = jnp.where(hit, lse, far_below)
        level = jnp.max(lse, axis=0)
        w = jnp.where(hit, jnp.exp(lse - level[None]), 0.0)
        den = jnp.sum(w, axis=0)
        some = den > 0.0
        den = jnp.where(some, den, 1.0)
        share = (w / den[None]).reshape(n * dec, 128)
        high = share.astype(jnp.bfloat16)
        low = (share - high.astype(jnp.float32)).astype(jnp.bfloat16)
        wide = jnp.dot(jnp.concatenate([high, low], axis=1), pick, preferred_element_type=jnp.float32)
        merged = jnp.sum(wide.reshape(n, dec, cols) * parts, axis=0)
        return merged.astype(jnp.bfloat16), jnp.where(some, level + jnp.log(den), far_below)

    for copy in copies1:
        copy.wait()

    count1 = inner_count * passages
    lse1 = stat1[:, :, 0].reshape(count1, dec, 128)
    slots1 = stat1[:, :, 1].reshape(count1, dec, 128)
    parts1 = part1[...].astype(jnp.float32).reshape(count1, dec, cols)
    copies2 = []
    for j in list(range(1, outer_count)) + [0]:
        target_outer = lax.rem(outer + j, outer_count)
        dst = target_outer * inner_count + inner
        merged, lse = merge(lse1, slots1 == dst.astype(jnp.float32), parts1)
        if j == 0:
            part3[outer] = merged
            stat3[outer] = lse
            continue
        part2[j] = merged
        stat2[j] = lse
        for i, (source, sink) in enumerate(((part2, part3), (stat2, stat3))):
            copies2.append(pltpu.make_async_remote_copy(
                src_ref=source.at[j], dst_ref=sink.at[outer], send_sem=send2.at[i, j], recv_sem=recv2.at[i, j],
                device_id=(dst, core), device_id_type=MESH))
            copies2[-1].start()
    for copy in copies2:
        copy.wait()

    lse3 = stat3[...]
    out[...] = merge(lse3, lse3 > 0.5 * far_below, part3[...].astype(jnp.float32))[0]


def local(dp, mp, store_rows, norm_gain, key_weight, value_weight, queries, counts, slot_plan):
    row_count, feats = store_rows.shape
    cols = key_weight.shape[1]
    width = min(256, cols)
    piece = min(512, feats)
    pieces = feats // piece
    passages = slot_plan.shape[0]
    dec = queries.shape[0]
    questions = counts.shape[0]
    inner = 1
    while inner * inner < dp and dp % (2 * inner) == 0:
        inner *= 2
    outer = dp // inner
    dims = (dp, mp, inner, row_count, feats, cols, piece, width, questions, dec, passages)
    vmem = pl.BlockSpec(memory_space=pltpu.VMEM)
    smem = pl.BlockSpec(memory_space=pltpu.SMEM)
    hbm = pl.BlockSpec(memory_space=pl.ANY)
    bf16, f32 = jnp.bfloat16, jnp.float32
    dma = pltpu.SemaphoreType.DMA
    return pl.pallas_call(
        functools.partial(body, dims),
        out_shape=jax.ShapeDtypeStruct((dec, cols), bf16),
        in_specs=[smem, smem, vmem, vmem, hbm, hbm, hbm],
        out_specs=vmem,
        scratch_shapes=[
            pltpu.VMEM((mp, row_count, feats), bf16),
            pltpu.VMEM((row_count, piece), bf16),
            pltpu.VMEM((mp, pieces, 2, piece, cols), bf16),
            pltpu.VMEM((2, row_count, cols), f32),
            pltpu.VMEM((2, row_count, cols), bf16),
            pltpu.VMEM((row_count, 1), f32),
            pltpu.VMEM((dp, dec, cols), bf16),
            pltpu.VMEM((inner, passages, dec, cols), bf16),
            pltpu.VMEM((inner, passages, 2, dec, 128), f32),
            pltpu.VMEM((outer, dec, cols), bf16),
            pltpu.VMEM((outer, dec, 128), f32),
            pltpu.VMEM((outer, dec, cols), bf16),
            pltpu.VMEM((outer, dec, 128), f32),
            dma((pieces,)),
            dma((mp, pieces, 2)),
            dma((mp, pieces)),
            dma((mp, pieces)),
            dma((dp,)),
            dma((dp,)),
            dma((2, inner)),
            dma((2, inner)),
            dma((2, outer)),
            dma((2, outer)),
        ],
        compiler_params=pltpu.CompilerParams(
            collective_id=0, has_side_effects=True, vmem_limit_bytes=56 * 1024 * 1024),
    )(counts, slot_plan, norm_gain.reshape(1, -1), queries, store_rows, key_weight, value_weight)


def solution(mesh):
    placed = (P("dp", "mp"), P(), P(None, "mp"), P(None, "mp"), P("dp", "mp"), P(), P("dp"))
    return jax.shard_map(
        functools.partial(local, mesh.shape["dp"], mesh.shape["mp"]),
        mesh=mesh, in_specs=placed, out_specs=P("dp", "mp"), check_vma=False
    )
```

time: 45.8 us -> 39.4 us (0.86)
  Pallas kernels: 42.8 us -> 36.3 us
    pallas_call x1, Pallas kernels: 42.8 us -> 36.3 us  [local(): pl.pallas_call(functools.partial(body, dims), out_shape=jax.ShapeDtypeStr...]
where the time goes in v2:
time: 39.4 us; the launch traced here: 39 us
  Pallas kernels  36.3 us (92%)
  local copies, waits for them, and re-layouts  2.64 us (7%)
    pallas_call x1, Pallas kernels, local(): pl.pallas_call(functools.partial(body, dims), out_shape=jax.ShapeDtypeStr...  36.3 us
    unnamed x1, local copies, waits for them, and re-layouts  1.32 us
    reshape x1, local copies, waits for them, and re-layouts, local(): norm_gain.reshape(1, -1)  1.31 us

profile of v2, /device:TPU:0, one launch (start us, length us, event | category | flops | bytes accessed | tf_op | source)
XLA Modules:
  0.0 39.0 jit_solution(10241175144994067817)
XLA Ops:
  0.0 1.3 %reshape.3.gain = bf16[1,4096]{1,0:T(2,128)(2,1)} reshape(bf16[4096]{0:T(1024)(128)(2,1)} %param.8) | data formatting | bytes 16384 | tf_op jit(solution)/shard_map/reshape | solution.py:271
  1.3 36.3 %shard_map.73 = bf16[8,1024]{1,0:T(8,128)(2,1)} custom-call(s32[16]{0:T(128)} %counts.1, s32[2]{0:T(128)} %plan.1, bf16[1,4096]{1,0:T(2,128)(2,1)} %reshape.3.gain, bf16[8,1024]{1,0:T(8,128)(2,1)} %queries.1, bf16[512,2048]{1,0:T(8,128)(2,1)} %rows_hbm.1, bf16[4096,1024]{1,0:T(8,128)(2,1)} %key_hbm.1, bf16[4096,1024]{1,0:T(8,128)(2,1)} %value_hbm.1), custom_call_target="tpu_custom_call" | custom-call | tf_op jit(solution)/shard_map/pallas_call | solution.py:239
  37.7 1.3 %copy.9 = bf16[8,1024]{1,0:T(8,128)(2,1)} copy(bf16[8,1024]{1,0:T(8,128)(2,1)} %shard_map.73) | data formatting | bytes 32768

commit v3 on v2

--- a/solution.py
+++ b/solution.py
@@ -81,13 +81,16 @@
 
     def scale(s, k):
         start = lax.rem(core + s, mp) * feats + k * piece
-        own_gain = gain[:, pl.ds(pl.multiple_of(start, piece), piece)].astype(jnp.float32)
+        own_gain = gain[pl.ds(pl.multiple_of(start, piece), piece)].astype(jnp.float32).reshape(1, piece)
 
         def step(i, carry):
             at = pl.ds(pl.multiple_of(i * row_step, row_step), row_step)
             x = raw[s, at, feature_span(k)].astype(jnp.float32)
             scaled[at, :] = (x * own_gain).astype(jnp.bfloat16)
-            total = jnp.sum(x * x, axis=1, keepdims=True)
+            square = x * x
+            total = square[:, :128]
+            for lanes in range(128, piece, 128):
+                total = total + square[:, lanes:lanes + 128]
             if s + k > 0:
                 total = total + sumsq[at, :]
             sumsq[at, :] = total
@@ -104,7 +107,7 @@
             scale(s, k)
             last = s == mp - 1 and k == pieces - 1
             if last:
-                inv_rms = lax.rsqrt(sumsq[...] * (1.0 / full) + norm_eps)
+                inv_rms = lax.rsqrt(jnp.sum(sumsq[...], axis=1, keepdims=True) * (1.0 / full) + norm_eps)
             for c in range(2):
                 weight_copy(s, k, c).wait()
                 product = jnp.dot(scaled[...], wbuf[s, k, c], preferred_element_type=jnp.float32)
@@ -247,7 +250,7 @@
             pltpu.VMEM((mp, pieces, 2, piece, cols), bf16),
             pltpu.VMEM((2, row_count, cols), f32),
             pltpu.VMEM((2, row_count, cols), bf16),
-            pltpu.VMEM((row_count, 1), f32),
+            pltpu.VMEM((row_count, 128), f32),
             pltpu.VMEM((dp, dec, cols), bf16),
             pltpu.VMEM((inner, passages, dec, cols), bf16),
             pltpu.VMEM((inner, passages, 2, dec, 128), f32),
@@ -268,7 +271,7 @@
         ],
         compiler_params=pltpu.CompilerParams(
             collective_id=0, has_side_effects=True, vmem_limit_bytes=56 * 1024 * 1024),
-    )(counts, slot_plan, norm_gain.reshape(1, -1), queries, store_rows, key_weight, value_weight)
+    )(counts, slot_plan, norm_gain, queries, store_rows, key_weight, value_weight)
 
 
 def solution(mesh):

time: 39.4 us -> 33.4 us (0.85)
  Pallas kernels: 36.3 us -> 31.8 us
  local copies, waits for them, and re-layouts: 2.64 us -> 1.32 us
    pallas_call x1, Pallas kernels: 36.3 us -> 31.8 us  [local(): pl.pallas_call(functools.partial(body, dims), out_shape=jax.ShapeDtypeStr...]
    reshape x1 -> x0, local copies, waits for them, and re-layouts: 1.31 us -> none  [local(): norm_gain.reshape(1, -1)]
where the time goes in v3:
time: 33.4 us; the launch traced here: 33.1 us
  Pallas kernels  31.8 us (95%)
  local copies, waits for them, and re-layouts  1.32 us (4%)
    pallas_call x1, Pallas kernels, local(): pl.pallas_call(functools.partial(body, dims), out_shape=jax.ShapeDtypeStr...  31.8 us
    unnamed x1, local copies, waits for them, and re-layouts  1.32 us

profile of v3, /device:TPU:0, one launch (start us, length us, event | category | flops | bytes accessed | tf_op | source)
XLA Modules:
  0.0 33.1 jit_solution(6617833948259141838)
XLA Ops:
  0.0 31.8 %shard_map.73 = bf16[8,1024]{1,0:T(8,128)(2,1)} custom-call(s32[16]{0:T(128)} %counts.1, s32[2]{0:T(128)} %plan.1, bf16[4096]{0:T(1024)(128)(2,1)} %gain.1, bf16[8,1024]{1,0:T(8,128)(2,1)} %queries.1, bf16[512,2048]{1,0:T(8,128)(2,1)} %rows_hbm.1, bf16[4096,1024]{1,0:T(8,128)(2,1)} %key_hbm.1, bf16[4096,1024]{1,0:T(8,128)(2,1)} %value_hbm.1), custom_call_target="tpu_custom_call" | custom-call | tf_op jit(solution)/shard_map/pallas_call | solution.py:242
  31.8 1.3 %copy.9 = bf16[8,1024]{1,0:T(8,128)(2,1)} copy(bf16[8,1024]{1,0:T(8,128)(2,1)} %shard_map.73) | data formatting | bytes 32768
